TPU v7x, 32 devices: a whole 2x2x4 slice. The times are simulated.
32 devices in a mesh: chan: 4 (over z), frame: 8 (over y, x, core).
Axes of the slice: x: 2, y: 2, z: 4, core: 2. Of those that a mesh axis runs over, the one named last changes fastest.
Arguments:
- rf_data: bfloat16 [2, 8, 256, 1024], P(None, None, 'frame', 'chan'), may hold values from -6 to 6
- elem_pos: int32 [3, 1024], replicated, may hold values from -16 to 15, as said below
- vox_pos: int32 [3, 4096], P(None, 'chan'), may hold values from -32 to 62, as said below
- subbands: int32 [8], replicated, may hold values from 0 to 63, as said below
Outputs:
- filtered: bfloat16 [256, 2, 8, 4096], P('frame', None, None, 'chan')
Inputs may be any that keep to these rules, and one draw needn't show every extreme that they name: `elem_pos`: the element positions are the 32 x 32 grid with x and y from -16, each point once in a drawn order; z is 0, 1 or 2. `vox_pos`: distinct voxels of a box: x and y from -32 to 31, z from 48 to 62 in steps of 2. `subbands`: 8 distinct bin numbers.
All inputs are finite; a program needn't handle non-finite values.
Results may differ from a plain program's by a relative error of at most 0.0075.
Values may be sent and summed in bfloat16 or wider, within the bound.
A program may use at most 128 MiB of HBM per device.

v0:
```python
import math

import jax
import jax.numpy as jnp
from jax import lax
from jax.sharding import PartitionSpec as P

TWO_PI = 2.0 * math.pi
EPSILON = 1e-06


def geometry(elem_pos, coords):
    elem = elem_pos.astype(jnp.float32)
    voxel = coords.astype(jnp.float32)
    delta_x = voxel[0][:, None] - elem[0][None, :]
    delta_y = voxel[1][:, None] - elem[1][None, :]
    delta_z = voxel[2][:, None] - elem[2][None, :]
    distance = jnp.sqrt(delta_x * delta_x + delta_y * delta_y + delta_z * delta_z)
    inverse = 1.0 / math.sqrt(elem_pos.shape[1])
    weight = delta_z / distance * inverse
    travel = voxel[2][:, None] + distance
    return (weight, travel)


def data_matrix(gathered):
    data_re = jnp.swapaxes(gathered[0], 1, 2)
    data_im = jnp.swapaxes(gathered[1], 1, 2)
    upper_rows = jnp.concatenate([data_re, data_im], axis=2)
    lower_rows = jnp.concatenate([-data_im, data_re], axis=2)
    return jnp.concatenate([upper_rows, lower_rows], axis=1)


def beamform(gathered, elem_pos, coords, subbands):
    weight, travel = geometry(elem_pos, coords)
    wavenum = (32.0 + subbands.astype(jnp.float32)) / 64.0
    matrix = data_matrix(gathered)
    nbins = gathered.shape[1]
    frames = gathered.shape[2]
    results = []
    for index in range(nbins):
        phase_angle = TWO_PI * wavenum[index] * travel
        operator = jnp.concatenate(
            [weight * jnp.cos(phase_angle), -(weight * jnp.sin(phase_angle))], axis=1
        ).astype(jnp.bfloat16)
        results.append(
            jnp.dot(operator, matrix[index], preferred_element_type=jnp.float32).astype(
                jnp.bfloat16
            )
        )
    volumes = jnp.stack(results, axis=1)
    return volumes.reshape(volumes.shape[0], nbins, 2, frames)


def complex_product(left_pair, right_pair):
    first_re, first_im = left_pair
    second_re, second_im = right_pair
    high = lax.Precision.HIGHEST
    real_part = jnp.einsum("bij,bjk->bik", first_re, second_re, precision=high) - jnp.einsum(
        "bij,bjk->bik", first_im, second_im, precision=high
    )
    imag_part = jnp.einsum("bij,bjk->bik", first_re, second_im, precision=high) + jnp.einsum(
        "bij,bjk->bik", first_im, second_re, precision=high
    )
    return (real_part, imag_part)


def filter_matrix(gram):
    gram_re = gram[:, 0]
    gram_im = gram[:, 1]
    frames = gram.shape[2]
    squares = jnp.sum(gram_re * gram_re + gram_im * gram_im, axis=(1, 2))
    factor = 4.0 / jnp.sqrt(squares + EPSILON)
    mat_re = gram_re * factor[:, None, None]
    mat_im = gram_im * factor[:, None, None]
    second = complex_product((mat_re, mat_im), (mat_re, mat_im))
    third = complex_product(second, (mat_re, mat_im))
    identity = jnp.eye(frames, dtype=jnp.float32)[None]
    filter_re = identity - mat_re + 0.3 * second[0] - 0.03 * third[0]
    filter_im = -mat_im + 0.3 * second[1] - 0.03 * third[1]
    return jnp.stack([filter_re, filter_im], axis=1).astype(jnp.bfloat16)


def block_filter(filter_bf):
    filter_re = filter_bf[:, 0]
    filter_im = filter_bf[:, 1]
    upper_rows = jnp.concatenate([filter_re, filter_im], axis=2)
    lower_rows = jnp.concatenate([-filter_im, filter_re], axis=2)
    return jnp.concatenate([upper_rows, lower_rows], axis=1)


def shards(rf_data, elem_pos, vox_pos, subbands):
    gathered = lax.all_gather(rf_data, "chan", axis=3, tiled=True)
    all_frames = lax.all_gather(gathered, "frame", axis=2, tiled=True)
    count = vox_pos.shape[1] // lax.axis_size("frame")
    offset = lax.axis_index("frame") * count
    coords = lax.dynamic_slice_in_dim(vox_pos, offset, count, 1)
    voxel_major = beamform(all_frames, elem_pos, coords, subbands)
    rows = voxel_major.shape[0]
    nbins = voxel_major.shape[1]
    frames = voxel_major.shape[3]
    stacked = voxel_major.reshape(rows, nbins, 2 * frames)
    products = jnp.einsum("vbi,vbj->bij", stacked, stacked, preferred_element_type=jnp.float32)
    gram_re = products[:, :frames, :frames] + products[:, frames:, frames:]
    gram_im = products[:, :frames, frames:] - products[:, frames:, :frames]
    gram = jnp.stack([gram_re, gram_im], axis=1)
    summed = lax.psum(gram, ("chan", "frame"))
    filter_bf = filter_matrix(summed)
    blocks = block_filter(filter_bf)
    applied = jnp.einsum(
        "vbi,bij->vbj", stacked, blocks, preferred_element_type=jnp.float32
    ).astype(jnp.bfloat16)
    applied = applied.reshape(rows, nbins, 2, frames)
    returned = lax.all_to_all(applied, "frame", split_axis=3, concat_axis=0, tiled=True)
    return jnp.transpose(returned, (3, 2, 1, 0))


def solution(mesh):
    return jax.shard_map(
        shards,
        mesh=mesh,
        in_specs=(P(None, None, "frame", "chan"), P(), P(None, "chan"), P()),
        out_specs=P("frame", None, None, "chan"),
        check_vma=False,
    )
```

profile of v0, /device:TPU:1, one launch (start us, length us, event | category | flops | bytes accessed | tf_op | source)
XLA Modules:
  0.0 310.3 jit_solution(17136735501208512236)
XLA Ops:
  6.5 0.7 all-gather.3.cloned.1.call-update
  7.3 32.3 %all-gather.3.cloned.1.call-done = bf16[2,8,32,1024]{3,2,1,0:T(8,128)(2,1)} async-done(((bf16[2,8,32,256]{3,2,1,0:T(8,128)(2,1)}), bf16[2,8,32,1024]{3,2,1,0:T(8,128)(2,1)}) %all-gather.3.cloned.1.call-update) | async-done | bytes 1048592 | tf_op jit(solution)/shard_map/all_gather | solution.py:92
  39.6 0.7 convert_element_type.57
  47.3 17.0 %multiply_convert_fusion = (bf16[128,1024]{1,0:T(8,128)(2,1)S(1)}, bf16[128,1024]{1,0:T(8,128)(2,1)}, bf16[128,1024]{1,0:T(8,128)(2,1)S(1)}, bf16[128,1024]{1,0:...) fusion(f32[]{:T(128)} %bitcast.33, ...), kind=kLoop, calls=%fused_computation.121 | loop fusion | flops 7733248 | bytes 4208160 | tf_op jit(solution)/shard_map/convert.4
  64.4 31.4 %all-gather.5.cloned.1.call-done = bf16[2,8,256,1024]{3,2,1,0:T(8,128)(2,1)} async-done(((bf16[2,8,32,1024]{3,2,1,0:T(8,128)(2,1)}), bf16[2,8,256,1024]{3,2,1,0:T(8,128)(2,1)}) %all-gather.5.cloned.1.call-update) | async-done | bytes 8388624 | tf_op jit(solution)/shard_map/all_gather | solution.py:93
  95.8 4.1 %slice_bitcast_fusion = (bf16[8,1024,256]{1,2,0:T(8,128)(2,1)S(1)}, bf16[8,1024,256]{1,2,0:T(8,128)(2,1)S(1)}) fusion(bf16[2,8,256,1024]{3,2,1,0:T(8,128)(2,1)} %all-gather.5.cloned.1.call-done), kind=kLoop, calls=%fused_computation.1 | loop fusion | bytes 16777216 | tf_op jit(solution)/shard_map/transpose | solution.py:27
  100.0 1.7 copy-done.1
  102.0 1.7 maximum_maximum_fusion
  103.8 0.8 fusion.64
  104.7 0.8 fusion.62
  105.7 0.8 fusion.60
  106.6 0.8 fusion.58
  107.4 0.8 fusion.56
  108.2 0.8 fusion.54
  109.1 0.8 fusion.52
  109.9 0.8 fusion.50
  110.8 1.3 fusion.129
  112.7 2.4 pad_maximum_fusion
  115.2 140.6 %all-reduce.2.cloned.1.call-done = f32[8,2,256,256]{3,2,0,1:T(8,128)} async-done(((f32[8,2,256,256]{3,2,0,1:T(8,128)}), f32[8,2,256,256]{3,2,0,1:T(8,128)}) %all-reduce.2.cloned.1.call-update) | async-done | bytes 4194320 | tf_op jit(solution)/shard_map/psum | solution.py:106
  255.7 2.8 add_reduce_fusion
  259.2 2.3 fusion.76
  261.5 2.3 fusion.71
  263.9 2.6 fusion.69
  266.5 2.3 fusion.67
  268.8 2.4 fusion.10
  271.2 2.4 fusion.8
  273.6 3.1 fusion.128
  276.7 3.3 %fusion.18 = bf16[8,256,256]{2,1,0:T(8,128)(2,1)S(1)} fusion(f32[8,256,256]{2,1,0:T(8,128)S(1)} %fusion.76, f32[8,256,256]{2,1,0:T(8,128)S(1)} %fusion.71, f32[8,256,256]{2,1,0:T(8,128)S(1)} %fusion.10, f32[8,2,256,256]{3,2,0,1:T(8,128)S(1)} %copy-done, f32[8]{0:T(128)S(1)} %rsqrt_multiply_fusion, f32[256,256]{1,0:T(8,128)S(1)} %fusion.115), kind=kOutput, calls=%fused_computation.24 | convolution fusion | flops 1616379904 | bytes 15991808 | tf_op jit(solution)/shard_map/bij,bjk->bik/dot_general | solution.py:58
  280.0 1.9 fusion.38
  281.9 1.1 copy.42
  283.0 19.5 %all_to_all.18 = bf16[128,8,2,256]{0,2,1,3:T(2,128)(2,1)S(1)} all-to-all(bf16[128,8,2,256]{0,2,1,3:T(2,128)(2,1)S(1)} %copy.42), channel_id=1, replica_groups=mesh['chan'=4,'frame'=8] {'frame'}, dimensions={3} | all-to-all | bytes 2097152 | tf_op jit(solution)/shard_map/all_to_all | solution.py:113
  302.5 1.2 copy.63
  (31 shorter events, 4.0 us)
Async XLA Ops:
  6.5 33.0 %all-gather.3.cloned.1.call-start = ((), (), s32[]{:S(2)}) async-start(), calls=%async_computation.1 | async-start | bytes 1310720 | tf_op jit(solution)/shard_map/all_gather | solution.py:92
  7.3 88.6 %all-gather.5.cloned.1.call-start = ((), (), s32[]{:S(2)}) async-start(), calls=%async_computation.2 | async-start | bytes 9437184 | tf_op jit(solution)/shard_map/all_gather | solution.py:93
  39.6 216.1 %all-reduce.2.cloned.1.call-start = ((), (), s32[]{:S(2)}) async-start(), calls=%async_computation.3 | async-start | bytes 8388608 | tf_op jit(solution)/shard_map/psum | solution.py:106
  95.8 5.8 %copy-start.1 = (bf16[2,8,256,1024]{3,2,1,0:T(8,128)(2,1)S(1)}, bf16[2,8,256,1024]{3,2,1,0:T(8,128)(2,1)}, u32[]{:S(2)}) copy-start(bf16[2,8,256,1024]{3,2,1,0:T(8,128)(2,1)} %all-gather.5.cloned.1.call-done) | copy-start | bytes 25165828
  102.0 1.8 copy-start.7
  102.0 1.8 copy-start.8
  103.7 1.0 copy-start.5
  103.7 1.0 copy-start.6
  104.6 1.0 copy-start.3
  104.6 1.1 copy-start.4
  105.6 1.0 copy-start.2
  255.7 3.4 %copy-start = (f32[8,2,256,256]{3,2,0,1:T(8,128)S(1)}, f32[8,2,256,256]{3,2,0,1:T(8,128)}, u32[]{:S(2)}) copy-start(f32[8,2,256,256]{3,2,0,1:T(8,128)} %all-reduce.2.cloned.1.call-done) | copy-start | bytes 12582916
Sparse Core Ops, SparseCore 0:
  8.9 30.6 all-gather.2
  41.5 54.3 all-gather.4
  115.2 140.4 all-reduce.1
where the time goes:
time: 312 us; the launch traced here: 310 us
  waiting for transfers between devices  205 us (66%)
  matrix products  30.6 us (10%)
  other arithmetic  26.9 us (9%)
  blocking collectives  19.5 us (6%)
  between operations  18.3 us (6%)
  local copies, waits for them, and re-layouts  9.73 us (3%)
    psum x1, waiting for transfers between devices, shards(): summed = lax.psum(gram, ('chan', 'frame'))  141 us
    all_gather x1, waiting for transfers between devices, shards(): gathered = lax.all_gather(rf_data, 'chan', axis=3, tiled=True)  32.3 us
    all_gather x1, waiting for transfers between devices, shards(): all_frames = lax.all_gather(gathered, 'frame', axis=2, tiled=True)  31.4 us
    all_to_all x1, blocking collectives, shards(): lax.all_to_all(applied, 'frame', split_axis=3, concat_axis=0, tiled=True)  19.5 us
    another operation x1, other arithmetic  17 us
    dot_general x8, matrix products, beamform(): jnp.dot(operator, matrix[index], preferred_element_type=jnp.float32)  6.67 us
  transfers between devices with their start and end apart: 3, of which 3 were waited for; matrix products, arithmetic and copies ran while one was open for 6% of the time, Pallas kernels for 0%

commit v1 on v0

v1 whole, which is shorter than its diff:
```python
import functools
import math

import jax
import jax.numpy as jnp
from jax import lax
from jax.experimental import pallas as pl
from jax.experimental.pallas import tpu as pltpu
from jax.sharding import PartitionSpec as P

EPSILON = 1e-06
MESH = pl.DeviceIdType.MESH
F32 = jnp.float32
BF16 = jnp.bfloat16
SIN_POLY = (
    3.1415927410125732, -5.167710304260254, 2.550077438354492,
    -0.598291277885437, 0.07765766233205795,
)
COS_POLY = (
    0.9999999403953552, -4.934792995452881, 4.058411121368408,
    -1.331876516342163, 0.21968960762023926,
)
LANES = 128
ROUND = 12582912.0


def horner(coefs, z):
    value = jnp.full_like(z, coefs[-1])
    for coef in coefs[-2::-1]:
        value = value * z + coef
    return value


def split(x):
    high = x.astype(BF16)
    return high, (x - high.astype(F32)).astype(BF16)


def dot(a, b):
    return jnp.dot(a, b, preferred_element_type=F32)


def dot_nt(a, b):
    return lax.dot_general(a, b, (((1,), (1,)), ((), ())), preferred_element_type=F32)


def kernel(
    nc, nf, nbins,
    rf_ref, elem_ref, vox_ref, sub_ref, out_ref,
    rfbuf, elem, vox, oper, acc, vols, part, slabs, total, sent,
    own_sem, plane_send, plane_recv, right_send, right_recv, left_send, left_recv,
    rs_send, rs_recv, ag_send, ag_recv, out_own, out_send, out_recv,
):
    share = nf // nbins
    frames = rfbuf.shape[2]
    cl = rfbuf.shape[3]
    chans = nc * cl
    vd = vols.shape[1]
    fl = frames // nf
    group = nc * share
    rows = frames // group
    me_c = lax.axis_index("chan")
    me_f = lax.axis_index("frame")
    me_bin = me_f // share
    me_sub = me_f % share
    me_g = me_c * share + me_sub

    def member(k):
        m = lax.rem(me_g + k, group)
        return m, (m // share, me_bin * share + m % share)

    def planar(k):
        j = lax.rem(me_f + k, nf)
        return j, (me_c, j)

    barrier = pltpu.get_barrier_semaphore()
    for k in range(1, nf):
        pl.semaphore_signal(barrier, inc=1, device_id=planar(k)[1], device_id_type=MESH)
    for k in range(1, nc):
        for s in range(share):
            other = (lax.rem(me_c + k, nc), me_bin * share + s)
            pl.semaphore_signal(barrier, inc=1, device_id=other, device_id_type=MESH)

    mine = pl.ds(pl.multiple_of(me_f * fl, fl), fl)
    own = pltpu.make_async_copy(rf_ref.at[:, me_bin], rfbuf.at[me_c, :, mine], own_sem)
    own.start()
    vstart = pl.multiple_of(me_sub * vd, LANES)
    vox[...] = vox_ref[:, pl.ds(vstart, vd)].astype(F32)
    for axis in range(3):
        for base in range(0, chans, LANES):
            row = elem_ref[axis:axis + 1, base:base + LANES].astype(F32)
            elem[axis, base:base + LANES, :] = jnp.broadcast_to(row, (LANES, LANES)).T
    pl.semaphore_wait(barrier, nf - 1 + (nc - 1) * share)

    def plane_copy(k):
        j, device = planar(k)
        return pltpu.make_async_remote_copy(
            src_ref=rf_ref.at[:, j // share], dst_ref=rfbuf.at[me_c, :, mine],
            send_sem=plane_send.at[j], recv_sem=plane_recv.at[me_f],
            device_id=device, device_id_type=MESH)

    def plane_arrival(k):
        j, device = planar(k)
        place = rfbuf.at[me_c, :, pl.ds(pl.multiple_of(j * fl, fl), fl)]
        return pltpu.make_async_remote_copy(
            src_ref=rf_ref.at[:, 0], dst_ref=place, send_sem=plane_send.at[j],
            recv_sem=plane_recv.at[j], device_id=device, device_id_type=MESH)

    for k in range(1, nf):
        plane_copy(k).start()

    wavenum = (32.0 + sub_ref[me_bin].astype(F32)) / 64.0
    inverse = 1.0 / math.sqrt(chans)

    def block_of(k):
        return lax.rem(me_c + k + nc, nc)

    def make_operator(block):
        @pl.loop(0, cl // 16)
        def _(step):
            place = pl.ds(pl.multiple_of(block * cl + step * 16, 16), 16)
            ex, ey, ez = elem[0, place, :], elem[1, place, :], elem[2, place, :]
            for base in range(0, vd, LANES):
                lanes = slice(base, base + LANES)
                vz = vox[2:3, lanes]
                dx, dy, dz = vox[0:1, lanes] - ex, vox[1:2, lanes] - ey, vz - ez
                square = dx * dx + dy * dy + dz * dz
                inv = lax.rsqrt(square)
                inv = inv * (1.5 - (0.5 * square) * (inv * inv))
                turns = wavenum * (vz + square * inv)
                turns = turns - ((turns + ROUND) - ROUND)
                z = turns * turns
                sine = turns * horner(SIN_POLY, z)
                cosine = horner(COS_POLY, z)
                weight = dz * inv * inverse
                twice = (weight + weight) * sine
                oper[0, place, lanes] = (weight - twice * sine).astype(BF16)
                oper[1, place, lanes] = (twice * cosine).astype(BF16)

    def multiply(block, first=False, last=False):
        place = pl.ds(pl.multiple_of(block * cl, cl), cl)
        real, imag = rfbuf[block, 0], rfbuf[block, 1]
        upper = jnp.concatenate([real, imag], axis=1)
        lower = jnp.concatenate([imag, -real], axis=1)
        width = min(256, vd)

        @pl.loop(0, vd // width)
        def _(step):
            lanes = pl.ds(pl.multiple_of(step * width, width), width)
            both = jnp.concatenate([oper[0, place, lanes], oper[1, place, lanes]], axis=0)
            for half, left in enumerate((upper, lower)):
                where = slice(half * frames, (half + 1) * frames)
                value = dot(left, both)
                if not first:
                    value = value + acc[where, lanes]
                if last:
                    vols[where, lanes] = value.astype(BF16)
                else:
                    acc[where, lanes] = value

    make_operator(me_c)
    own.wait()
    for k in range(1, nf):
        plane_arrival(k).wait_recv()

    right = (lax.rem(me_c + 1, nc), me_f)
    left = (lax.rem(me_c + nc - 1, nc), me_f)
    steps = nc // 2

    def ring_copy(step, rightward, arriving):
        sign = -1 if rightward else 1
        block = block_of(sign * (step if arriving else step - 1))
        ref = rfbuf.at[block]
        if step == steps:
            ref = rfbuf.at[block, 0 if rightward else 1]
        sends, recvs = (right_send, right_recv) if rightward else (left_send, left_recv)
        return pltpu.make_async_remote_copy(
            src_ref=ref, dst_ref=ref, send_sem=sends.at[step - 1], recv_sem=recvs.at[step - 1],
            device_id=right if rightward else left, device_id_type=MESH)

    for step in range(1, steps + 1):
        for rightward in (True, False):
            ring_copy(step, rightward, False).start()
        if step < steps:
            make_operator(block_of(-step))
            make_operator(block_of(step))
        else:
            make_operator(block_of(steps))
        if step == 1:
            multiply(me_c, first=True)
        else:
            multiply(block_of(1 - step))
            multiply(block_of(step - 1))
        for rightward in (True, False):
            ring_copy(step, rightward, True).wait_recv()
    multiply(block_of(steps), last=True)

    real, imag = vols[:frames, :], vols[frames:, :]
    both = jnp.concatenate([real, imag], axis=1)
    gram_re = dot_nt(both, both)
    gram_im = dot_nt(jnp.concatenate([real, -imag], axis=1), jnp.concatenate([imag, real], axis=1))
    across = lax.broadcasted_iota(jnp.int32, (frames, frames), 1)
    down = lax.broadcasted_iota(jnp.int32, (frames, frames), 0)
    part[...] = jnp.where(down <= across, gram_re, gram_im)

    def slab_of(m):
        return pl.ds(pl.multiple_of(m * rows, rows), rows)

    def scatter(k):
        m, device = member(k)
        return pltpu.make_async_remote_copy(
            src_ref=part.at[slab_of(m)], dst_ref=slabs.at[me_g],
            send_sem=rs_send.at[m], recv_sem=rs_recv.at[me_g],
            device_id=device, device_id_type=MESH)

    def scatter_arrival(k):
        m, device = member(k)
        return pltpu.make_async_remote_copy(
            src_ref=part.at[slab_of(m)], dst_ref=slabs.at[m],
            send_sem=rs_send.at[m], recv_sem=rs_recv.at[m],
            device_id=device, device_id_type=MESH)

    def gather(k, arriving=False):
        m, device = member(k)
        source = m if arriving else me_g
        return pltpu.make_async_remote_copy(
            src_ref=total.at[slab_of(source)], dst_ref=total.at[slab_of(source)],
            send_sem=ag_send.at[m], recv_sem=ag_recv.at[source],
            device_id=device, device_id_type=MESH)

    for k in range(1, group):
        scatter(k).start()
    summed = part[slab_of(me_g), :]
    for k in range(1, group):
        scatter_arrival(k).wait_recv()
        summed = summed + slabs[member(k)[0]]
    total[slab_of(me_g), :] = summed
    for k in range(1, group):
        gather(k).start()
    for k in range(1, group):
        gather(k, True).wait_recv()

    packed = total[...]
    turned = packed.T
    mat_re = jnp.where(down <= across, packed, turned)
    mat_im = jnp.where(down > across, packed, jnp.where(down < across, -turned, 0.0))
    squares = jnp.sum(jnp.sum(mat_re * mat_re + mat_im * mat_im, axis=1, keepdims=True), axis=0, keepdims=True)
    factor = 4.0 / jnp.sqrt(squares + EPSILON)
    mat_re = mat_re * factor
    mat_im = mat_im * factor
    rhs = jnp.concatenate(
        [jnp.concatenate([mat_re, mat_im], axis=1), jnp.concatenate([-mat_im, mat_re], axis=1)], axis=0)
    rhs_high, rhs_low = split(rhs)

    def product(pair):
        high, low = split(pair)
        return dot(high, rhs_high) + (dot(high, rhs_low) + dot(low, rhs_high))

    first = jnp.concatenate([mat_re, mat_im], axis=1)
    second = product(first)
    third = product(second)
    poly = 0.3 * second - 0.03 * third - first
    acc[:frames, :frames] = jnp.where(down == across, 1.0, 0.0) + poly[:, :frames]
    acc[frames:, :frames] = poly[:, frames:]

    def out_copy(j):
        return pltpu.make_async_remote_copy(
            src_ref=sent.at[:, pl.ds(pl.multiple_of(j * fl, fl), fl)], dst_ref=out_ref.at[me_f],
            send_sem=out_send.at[j], recv_sem=out_recv.at[me_f],
            device_id=(me_c, j), device_id_type=MESH)

    chunks = 4
    per = nf // chunks
    height = per * fl
    my_chunk = me_f // per
    for step in range(1, chunks + 1):
        chunk = lax.rem(my_chunk + step, chunks)
        place = pl.ds(pl.multiple_of(chunk * height, height), height)
        below = pl.ds(pl.multiple_of(frames + chunk * height, height), height)
        h_re = acc[place, :frames].astype(BF16)
        h_im = acc[below, :frames].astype(BF16)
        lhs = jnp.concatenate(
            [jnp.concatenate([h_re, h_im], axis=1), jnp.concatenate([-h_im, h_re], axis=1)], axis=0)
        value = dot(lhs, vols[...]).astype(BF16)
        sent[0, place, :] = value[:height]
        sent[1, place, :] = value[height:]
        for q in range(per):
            j = chunk * per + q
            if step < chunks:
                out_copy(j).start()
            else:
                @pl.when(j != me_f)
                def _():
                    out_copy(j).start()
    own_out = pltpu.make_async_copy(sent.at[:, mine], out_ref.at[me_f], out_own)
    own_out.start()
    for k in range(1, nf):
        plane_copy(k).wait_send()
    for step in range(1, steps + 1):
        for rightward in (True, False):
            ring_copy(step, rightward, False).wait_send()
    for k in range(1, group):
        scatter(k).wait_send()
        gather(k).wait_send()
    own_out.wait()
    for k in range(1, nf):
        j, device = planar(k)
        pltpu.make_async_remote_copy(
            src_ref=sent.at[:, mine], dst_ref=out_ref.at[j], send_sem=out_send.at[j],
            recv_sem=out_recv.at[j], device_id=device, device_id_type=MESH).wait()


def shards(nc, nf, rf_data, elem_pos, vox_pos, subbands):
    nbins, fl, cl = rf_data.shape[1:]
    frames = fl * nf
    chans = cl * nc
    share = nf // nbins
    vl = vox_pos.shape[1]
    vd = vl // share
    group = nc * share
    steps = nc // 2
    dma = pltpu.SemaphoreType.DMA
    vmem = pl.BlockSpec(memory_space=pltpu.VMEM)
    received = pl.pallas_call(
        functools.partial(kernel, nc, nf, nbins),
        out_shape=jax.ShapeDtypeStruct((nf, 2, fl, vd), BF16),
        in_specs=[vmem, vmem, vmem, pl.BlockSpec(memory_space=pltpu.SMEM)],
        out_specs=pl.BlockSpec(memory_space=pl.ANY),
        scratch_shapes=[
            pltpu.VMEM((nc, 2, frames, cl), BF16),
            pltpu.VMEM((3, chans, LANES), F32),
            pltpu.VMEM((3, vd), F32),
            pltpu.VMEM((2, chans, vd), BF16),
            pltpu.VMEM((2 * frames, vd), F32),
            pltpu.VMEM((2 * frames, vd), BF16),
            pltpu.VMEM((frames, frames), F32),
            pltpu.VMEM((group, frames // group, frames), F32),
            pltpu.VMEM((frames, frames), F32),
            pltpu.VMEM((2, frames, vd), BF16),
            dma, dma((nf,)), dma((nf,)),
            dma((steps,)), dma((steps,)), dma((steps,)), dma((steps,)),
            dma((group,)), dma((group,)), dma((group,)), dma((group,)),
            dma, dma((nf,)), dma((nf,)),
        ],
        compiler_params=pltpu.CompilerParams(
            collective_id=0, has_side_effects=True, vmem_limit_bytes=48 * 2**20),
    )(rf_data, elem_pos, vox_pos, subbands)
    received = received.reshape(nbins, share, 2, fl, vd)
    return jnp.transpose(received, (3, 2, 0, 1, 4)).reshape(fl, 2, nbins, vl)


def solution(mesh):
    return jax.shard_map(
        functools.partial(shards, mesh.shape["chan"], mesh.shape["frame"]),
        mesh=mesh,
        in_specs=(P(None, None, "frame", "chan"), P(), P(None, "chan"), P()),
        out_specs=P("frame", None, None, "chan"),
        check_vma=False,
    )
```

time: 312 us -> 65.5 us (0.21)
  the two profiles are of different devices: /device:TPU:1 before, /device:TPU:25 now
where the time goes in v1:
time: 65.5 us; the launch traced here: 65.2 us
  Pallas kernels  60.6 us (93%)
  local copies, waits for them, and re-layouts  4.59 us (7%)
    pallas_call x1, Pallas kernels, shards(): pl.pallas_call(functools.partial(kernel, nc, nf, nbins), out_shape=jax.Sh...  60.6 us
    unnamed x8, local copies, waits for them, and re-layouts  3.04 us
    reshape x1, local copies, waits for them, and re-layouts, shards(): return jnp.transpose(received, (3, 2, 0, 1, 4)).reshape(fl, 2, nbins, vl)  1.55 us

profile of v1, /device:TPU:25, one launch (start us, length us, event | category | flops | bytes accessed | tf_op | source)
XLA Modules:
  0.0 65.2 jit_solution(17930360323843056751)
XLA Ops:
  0.0 0.0 copy-start
  0.0 0.9 %copy-done = bf16[2,8,32,256]{3,2,1,0:T(8,128)(2,1)S(1)} copy-done((bf16[2,8,32,256]{3,2,1,0:T(8,128)(2,1)S(1)}, bf16[2,8,32,256]{3,2,1,0:T(8,128)(2,1)}, u32[]{:S(2)}) %copy-start) | copy-done | bytes 262168
  1.0 0.0 copy-start.1
  1.0 0.7 %copy-done.1 = s32[3,1024]{1,0:T(4,128)S(1)} copy-done((s32[3,1024]{1,0:T(4,128)S(1)}, s32[3,1024]{1,0:T(4,128)}, u32[]{:S(2)}) %copy-start.1) | copy-done | bytes 12312
  1.7 0.0 copy-start.2
  1.7 0.7 %copy-done.2 = s32[3,1024]{1,0:T(4,128)S(1)} copy-done((s32[3,1024]{1,0:T(4,128)S(1)}, s32[3,1024]{1,0:T(4,128)}, u32[]{:S(2)}) %copy-start.2) | copy-done | bytes 12312
  2.4 0.0 copy-start.3
  2.4 0.7 %copy-done.3 = s32[8]{0:T(128)S(1)} copy-done((s32[8]{0:T(128)S(1)}, s32[8]{0:T(128)}, u32[]{:S(2)}) %copy-start.3) | copy-done | bytes 56
  3.0 60.6 %shard_map.46 = bf16[8,2,32,1024]{3,2,1,0:T(8,128)(2,1)S(1)} custom-call(bf16[2,8,32,256]{3,2,1,0:T(8,128)(2,1)S(1)} %copy-done, s32[3,1024]{1,0:T(4,128)S(1)} %copy-done.1, s32[3,1024]{1,0:T(4,128)S(1)} %copy-done.2, s32[8]{0:T(128)S(1)} %copy-done.3), custom_call_target="tpu_custom_call" | custom-call | tf_op jit(solution)/shard_map/pallas_call | solution.py:324
  63.6 1.5 %copy.5 = bf16[32,2,8,1024]{3,2,1,0:T(8,128)(2,1)} copy(bf16[32,2,8,1024]{3,0,1,2:T(8,128)(2,1)S(1)} %bitcast.5) | data formatting | bytes 2097152 | tf_op jit(solution)/shard_map/reshape | solution.py:349
Async XLA Ops:
  0.0 0.9 %copy-start = (bf16[2,8,32,256]{3,2,1,0:T(8,128)(2,1)S(1)}, bf16[2,8,32,256]{3,2,1,0:T(8,128)(2,1)}, u32[]{:S(2)}) copy-start(bf16[2,8,32,256]{3,2,1,0:T(8,128)(2,1)} %rf_ref.1) | copy-start | bytes 786436
  1.0 0.7 %copy-start.1 = (s32[3,1024]{1,0:T(4,128)S(1)}, s32[3,1024]{1,0:T(4,128)}, u32[]{:S(2)}) copy-start(s32[3,1024]{1,0:T(4,128)} %elem_ref.1) | copy-start | bytes 36868
  1.7 0.7 %copy-start.2 = (s32[3,1024]{1,0:T(4,128)S(1)}, s32[3,1024]{1,0:T(4,128)}, u32[]{:S(2)}) copy-start(s32[3,1024]{1,0:T(4,128)} %vox_ref.1) | copy-start | bytes 36868
  2.4 0.7 %copy-start.3 = (s32[8]{0:T(128)S(1)}, s32[8]{0:T(128)}, u32[]{:S(2)}) copy-start(s32[8]{0:T(128)} %sub_ref.1) | copy-start | bytes 100

commit v2 on v1

--- a/solution.py
+++ b/solution.py
@@ -46,8 +46,8 @@
 
 def kernel(
     nc, nf, nbins,
-    rf_ref, elem_ref, vox_ref, sub_ref, out_ref,
-    rfbuf, elem, vox, oper, acc, vols, part, slabs, total, sent,
+    rf_ref, elem_hbm, vox_hbm, sub_hbm, out_ref,
+    rfbuf, elem_ref, vox_ref, sub_ref, in_sem, elem, vox, oper, acc, vols, part, slabs, total, sent,
     own_sem, plane_send, plane_recv, right_send, right_recv, left_send, left_recv,
     rs_send, rs_recv, ag_send, ag_recv, out_own, out_send, out_recv,
 ):
@@ -81,15 +81,20 @@
             other = (lax.rem(me_c + k, nc), me_bin * share + s)
             pl.semaphore_signal(barrier, inc=1, device_id=other, device_id_type=MESH)
 
-    mine = pl.ds(pl.multiple_of(me_f * fl, fl), fl)
+    def piece(j):
+        return pl.ds(pl.multiple_of(j * fl, fl), fl)
+
+    mine = piece(me_f)
     own = pltpu.make_async_copy(rf_ref.at[:, me_bin], rfbuf.at[me_c, :, mine], own_sem)
     own.start()
-    vstart = pl.multiple_of(me_sub * vd, LANES)
-    vox[...] = vox_ref[:, pl.ds(vstart, vd)].astype(F32)
-    for axis in range(3):
-        for base in range(0, chans, LANES):
-            row = elem_ref[axis:axis + 1, base:base + LANES].astype(F32)
-            elem[axis, base:base + LANES, :] = jnp.broadcast_to(row, (LANES, LANES)).T
+    loads = [
+        pltpu.make_async_copy(source, place, in_sem.at[index])
+        for index, (source, place) in enumerate(
+            ((elem_hbm, elem_ref), (vox_hbm, vox_ref), (sub_hbm, sub_ref)))
+    ]
+    for load in loads:
+        load.start()
+    own.wait()
     pl.semaphore_wait(barrier, nf - 1 + (nc - 1) * share)
 
     def plane_copy(k):
@@ -99,26 +104,23 @@
             send_sem=plane_send.at[j], recv_sem=plane_recv.at[me_f],
             device_id=device, device_id_type=MESH)
 
-    def plane_arrival(k):
-        j, device = planar(k)
-        place = rfbuf.at[me_c, :, pl.ds(pl.multiple_of(j * fl, fl), fl)]
-        return pltpu.make_async_remote_copy(
-            src_ref=rf_ref.at[:, 0], dst_ref=place, send_sem=plane_send.at[j],
-            recv_sem=plane_recv.at[j], device_id=device, device_id_type=MESH)
+    def plane_arrival(j):
+        return pltpu.make_async_remote_copy(
+            src_ref=rf_ref.at[:, 0], dst_ref=rfbuf.at[me_c, :, piece(j)], send_sem=plane_send.at[j],
+            recv_sem=plane_recv.at[j], device_id=(me_c, j), device_id_type=MESH)
 
     for k in range(1, nf):
         plane_copy(k).start()
 
-    wavenum = (32.0 + sub_ref[me_bin].astype(F32)) / 64.0
     inverse = 1.0 / math.sqrt(chans)
 
     def block_of(k):
         return lax.rem(me_c + k + nc, nc)
 
-    def make_operator(block):
-        @pl.loop(0, cl // 16)
+    def make_operator(block, offset, count):
+        @pl.loop(0, count)
         def _(step):
-            place = pl.ds(pl.multiple_of(block * cl + step * 16, 16), 16)
+            place = pl.ds(pl.multiple_of(block * cl + (offset + step) * 16, 16), 16)
             ex, ey, ez = elem[0, place, :], elem[1, place, :], elem[2, place, :]
             for base in range(0, vd, LANES):
                 lanes = slice(base, base + LANES)
@@ -158,41 +160,81 @@
                 else:
                     acc[where, lanes] = value
 
-    make_operator(me_c)
-    own.wait()
-    for k in range(1, nf):
-        plane_arrival(k).wait_recv()
-
     right = (lax.rem(me_c + 1, nc), me_f)
     left = (lax.rem(me_c + nc - 1, nc), me_f)
     steps = nc // 2
 
-    def ring_copy(step, rightward, arriving):
+    def ring_copy(step, j, rightward, arriving):
         sign = -1 if rightward else 1
         block = block_of(sign * (step if arriving else step - 1))
-        ref = rfbuf.at[block]
+        ref = rfbuf.at[block, :, piece(j)]
         if step == steps:
-            ref = rfbuf.at[block, 0 if rightward else 1]
+            ref = rfbuf.at[block, 0 if rightward else 1, piece(j)]
         sends, recvs = (right_send, right_recv) if rightward else (left_send, left_recv)
-        return pltpu.make_async_remote_copy(
-            src_ref=ref, dst_ref=ref, send_sem=sends.at[step - 1], recv_sem=recvs.at[step - 1],
+        index = (step - 1) * nf + j
+        return pltpu.make_async_remote_copy(
+            src_ref=ref, dst_ref=ref, send_sem=sends.at[index], recv_sem=recvs.at[index],
             device_id=right if rightward else left, device_id_type=MESH)
 
-    for step in range(1, steps + 1):
+    for rightward in (True, False):
+        ring_copy(1, me_f, rightward, False).start()
+
+    for load in loads:
+        load.wait()
+    vstart = pl.multiple_of(me_sub * vd, LANES)
+    vox[...] = vox_ref[:, pl.ds(vstart, vd)].astype(F32)
+    for axis in range(3):
+        for base in range(0, chans, LANES):
+            row = elem_ref[axis:axis + 1, base:base + LANES].astype(F32)
+            elem[axis, base:base + LANES, :] = jnp.broadcast_to(row, (LANES, LANES)).T
+    wavenum = (32.0 + sub_ref[me_bin].astype(F32)) / 64.0
+
+    tall = cl // 16
+    portion = 2 * tall // nf
+
+    def portion_of_operator(phase, k):
+        at = k * portion
+        later = at >= tall
+        block = jnp.where(later, block_of(-phase - 1), block_of(phase))
+        make_operator(block, jnp.where(later, at - tall, at), portion)
+
+    portion_of_operator(0, 0)
+
+    @pl.loop(1, nf)
+    def _(k):
+        j = lax.rem(me_f - k + nf, nf)
+        plane_arrival(j).wait_recv()
         for rightward in (True, False):
-            ring_copy(step, rightward, False).start()
-        if step < steps:
-            make_operator(block_of(-step))
-            make_operator(block_of(step))
-        else:
-            make_operator(block_of(steps))
+            ring_copy(1, j, rightward, False).start()
+        portion_of_operator(0, k)
+
+    for step in range(1, steps):
         if step == 1:
             multiply(me_c, first=True)
         else:
             multiply(block_of(1 - step))
             multiply(block_of(step - 1))
+
+        @pl.loop(0, nf)
+        def _(k):
+            j = lax.rem(me_f - k + nf, nf)
+            for rightward in (True, False):
+                ring_copy(step, j, rightward, True).wait_recv()
+                ring_copy(step + 1, j, rightward, False).start()
+            portion_of_operator(step, k)
+
+    if steps == 1:
+        multiply(me_c, first=True)
+    else:
+        multiply(block_of(1 - steps))
+        multiply(block_of(steps - 1))
+
+    @pl.loop(0, nf)
+    def _(k):
+        j = lax.rem(me_f - k + nf, nf)
         for rightward in (True, False):
-            ring_copy(step, rightward, True).wait_recv()
+            ring_copy(steps, j, rightward, True).wait_recv()
+
     multiply(block_of(steps), last=True)
 
     real, imag = vols[:frames, :], vols[frames:, :]
@@ -201,7 +243,7 @@
     gram_im = dot_nt(jnp.concatenate([real, -imag], axis=1), jnp.concatenate([imag, real], axis=1))
     across = lax.broadcasted_iota(jnp.int32, (frames, frames), 1)
     down = lax.broadcasted_iota(jnp.int32, (frames, frames), 0)
-    part[...] = jnp.where(down <= across, gram_re, gram_im)
+    part[...] = jnp.where(down <= across, gram_re, gram_im).astype(BF16)
 
     def slab_of(m):
         return pl.ds(pl.multiple_of(m * rows, rows), rows)
@@ -230,17 +272,17 @@
 
     for k in range(1, group):
         scatter(k).start()
-    summed = part[slab_of(me_g), :]
+    summed = part[slab_of(me_g), :].astype(F32)
     for k in range(1, group):
         scatter_arrival(k).wait_recv()
-        summed = summed + slabs[member(k)[0]]
-    total[slab_of(me_g), :] = summed
+        summed = summed + slabs[member(k)[0]].astype(F32)
+    total[slab_of(me_g), :] = summed.astype(BF16)
     for k in range(1, group):
         gather(k).start()
     for k in range(1, group):
         gather(k, True).wait_recv()
 
-    packed = total[...]
+    packed = total[...].astype(F32)
     turned = packed.T
     mat_re = jnp.where(down <= across, packed, turned)
     mat_im = jnp.where(down > across, packed, jnp.where(down < across, -turned, 0.0))
@@ -297,8 +339,11 @@
     for k in range(1, nf):
         plane_copy(k).wait_send()
     for step in range(1, steps + 1):
-        for rightward in (True, False):
-            ring_copy(step, rightward, False).wait_send()
+        @pl.loop(0, nf)
+        def _(j):
+            for rightward in (True, False):
+                ring_copy(step, j, rightward, False).wait_send()
+
     for k in range(1, group):
         scatter(k).wait_send()
         gather(k).wait_send()
@@ -320,30 +365,33 @@
     group = nc * share
     steps = nc // 2
     dma = pltpu.SemaphoreType.DMA
-    vmem = pl.BlockSpec(memory_space=pltpu.VMEM)
     received = pl.pallas_call(
         functools.partial(kernel, nc, nf, nbins),
         out_shape=jax.ShapeDtypeStruct((nf, 2, fl, vd), BF16),
-        in_specs=[vmem, vmem, vmem, pl.BlockSpec(memory_space=pltpu.SMEM)],
+        in_specs=[pl.BlockSpec(memory_space=pl.ANY)] * 4,
         out_specs=pl.BlockSpec(memory_space=pl.ANY),
         scratch_shapes=[
             pltpu.VMEM((nc, 2, frames, cl), BF16),
+            pltpu.VMEM(elem_pos.shape, elem_pos.dtype),
+            pltpu.VMEM(vox_pos.shape, vox_pos.dtype),
+            pltpu.SMEM(subbands.shape, subbands.dtype),
+            dma((3,)),
             pltpu.VMEM((3, chans, LANES), F32),
             pltpu.VMEM((3, vd), F32),
             pltpu.VMEM((2, chans, vd), BF16),
             pltpu.VMEM((2 * frames, vd), F32),
             pltpu.VMEM((2 * frames, vd), BF16),
-            pltpu.VMEM((frames, frames), F32),
-            pltpu.VMEM((group, frames // group, frames), F32),
-            pltpu.VMEM((frames, frames), F32),
+            pltpu.VMEM((frames, frames), BF16),
+            pltpu.VMEM((group, frames // group, frames), BF16),
+            pltpu.VMEM((frames, frames), BF16),
             pltpu.VMEM((2, frames, vd), BF16),
             dma, dma((nf,)), dma((nf,)),
-            dma((steps,)), dma((steps,)), dma((steps,)), dma((steps,)),
+            dma((steps * nf,)), dma((steps * nf,)), dma((steps * nf,)), dma((steps * nf,)),
             dma((group,)), dma((group,)), dma((group,)), dma((group,)),
             dma, dma((nf,)), dma((nf,)),
         ],
         compiler_params=pltpu.CompilerParams(
-            collective_id=0, has_side_effects=True, vmem_limit_bytes=48 * 2**20),
+            collective_id=0, has_side_effects=True, vmem_limit_bytes=60 * 2**20),
     )(rf_data, elem_pos, vox_pos, subbands)
     received = received.reshape(nbins, share, 2, fl, vd)
     return jnp.transpose(received, (3, 2, 0, 1, 4)).reshape(fl, 2, nbins, vl)

time: 65.5 us -> 52.1 us (0.80)
  the two profiles are of different devices: /device:TPU:25 before, /device:TPU:1 now
where the time goes in v2:
time: 52.1 us; the launch traced here: 51.9 us
  Pallas kernels  49.1 us (94%)
  local copies, waits for them, and re-layouts  2.77 us (5%)
    pallas_call x1, Pallas kernels, shards(): pl.pallas_call(functools.partial(kernel, nc, nf, nbins), out_shape=jax.Sh...  49.1 us
    reshape x1, local copies, waits for them, and re-layouts, shards(): return jnp.transpose(received, (3, 2, 0, 1, 4)).reshape(fl, 2, nbins, vl)  2.77 us

profile of v2, /device:TPU:1, one launch (start us, length us, event | category | flops | bytes accessed | tf_op | source)
XLA Modules:
  0.0 51.9 jit_solution(17798193337821108816)
XLA Ops:
  0.0 49.1 %shard_map.46 = bf16[8,2,32,1024]{3,2,1,0:T(8,128)(2,1)} custom-call(bf16[2,8,32,256]{3,2,1,0:T(8,128)(2,1)} %rf_ref.1, s32[3,1024]{1,0:T(4,128)} %elem_hbm.1, s32[3,1024]{1,0:T(4,128)} %vox_hbm.1, s32[8]{0:T(128)} %sub_hbm.1), custom_call_target="tpu_custom_call" | custom-call | tf_op jit(solution)/shard_map/pallas_call | solution.py:368
  49.1 2.8 %copy.5 = bf16[32,2,8,1024]{3,2,1,0:T(8,128)(2,1)} copy(bf16[32,2,8,1024]{3,0,1,2:T(8,128)(2,1)} %bitcast.5) | data formatting | bytes 2097152 | tf_op jit(solution)/shard_map/reshape | solution.py:397

commit v3 on v2

--- a/solution.py
+++ b/solution.py
@@ -22,6 +22,7 @@
 )
 LANES = 128
 ROUND = 12582912.0
+GO_AT = 4
 
 
 def horner(coefs, z):
@@ -48,7 +49,7 @@
     nc, nf, nbins,
     rf_ref, elem_hbm, vox_hbm, sub_hbm, out_ref,
     rfbuf, elem_ref, vox_ref, sub_ref, in_sem, elem, vox, oper, acc, vols, part, slabs, total, sent,
-    own_sem, plane_send, plane_recv, right_send, right_recv, left_send, left_recv,
+    go_sem, own_sem, plane_send, plane_recv, right_send, right_recv, left_send, left_recv,
     rs_send, rs_recv, ag_send, ag_recv, out_own, out_send, out_recv,
 ):
     share = nf // nbins
@@ -176,9 +177,23 @@
             src_ref=ref, dst_ref=ref, send_sem=sends.at[index], recv_sem=recvs.at[index],
             device_id=right if rightward else left, device_id_type=MESH)
 
-    for rightward in (True, False):
-        ring_copy(1, me_f, rightward, False).start()
-
+    stagger = share == 1 and nf % 2 == 0
+    second = lax.rem(me_f, 2) == 1
+
+    def unless_second(run):
+        if stagger:
+            pl.when(jnp.logical_not(second))(run)
+        else:
+            run()
+
+    def send_own():
+        for rightward in (True, False):
+            ring_copy(1, me_f, rightward, False).start()
+
+    def let_go():
+        pl.semaphore_signal(go_sem, inc=1, device_id=(me_c, me_f + 1), device_id_type=MESH)
+
+    unless_second(send_own)
     for load in loads:
         load.wait()
     vstart = pl.multiple_of(me_sub * vd, LANES)
@@ -198,7 +213,14 @@
         block = jnp.where(later, block_of(-phase - 1), block_of(phase))
         make_operator(block, jnp.where(later, at - tall, at), portion)
 
-    portion_of_operator(0, 0)
+    if stagger:
+        @pl.when(second)
+        def _():
+            make_operator(0, 0, nc * tall)
+            pl.semaphore_wait(go_sem, 1)
+            send_own()
+
+    unless_second(lambda: portion_of_operator(0, 0))
 
     @pl.loop(1, nf)
     def _(k):
@@ -206,7 +228,10 @@
         plane_arrival(j).wait_recv()
         for rightward in (True, False):
             ring_copy(1, j, rightward, False).start()
-        portion_of_operator(0, k)
+        unless_second(lambda: portion_of_operator(0, k))
+
+    if stagger and steps == 1:
+        unless_second(let_go)
 
     for step in range(1, steps):
         if step == 1:
@@ -221,7 +246,12 @@
             for rightward in (True, False):
                 ring_copy(step, j, rightward, True).wait_recv()
                 ring_copy(step + 1, j, rightward, False).start()
-            portion_of_operator(step, k)
+            if stagger and step == steps - 1:
+                @pl.when(jnp.logical_and(jnp.logical_not(second), k == GO_AT * nf // 8))
+                def _():
+                    let_go()
+
+            unless_second(lambda: portion_of_operator(step, k))
 
     if steps == 1:
         multiply(me_c, first=True)
@@ -385,7 +415,7 @@
             pltpu.VMEM((group, frames // group, frames), BF16),
             pltpu.VMEM((frames, frames), BF16),
             pltpu.VMEM((2, frames, vd), BF16),
-            dma, dma((nf,)), dma((nf,)),
+            pltpu.SemaphoreType.REGULAR, dma, dma((nf,)), dma((nf,)),
             dma((steps * nf,)), dma((steps * nf,)), dma((steps * nf,)), dma((steps * nf,)),
             dma((group,)), dma((group,)), dma((group,)), dma((group,)),
             dma, dma((nf,)), dma((nf,)),

time: 52.1 us -> 51.4 us (0.987)
  Pallas kernels: 49.1 us -> 48.4 us
    pallas_call x1, Pallas kernels: 49.1 us -> 48.4 us  [shards(): pl.pallas_call(functools.partial(kernel, nc, nf, nbins), out_shape=jax.Sh...]
where the time goes in v3:
time: 51.4 us; the launch traced here: 51.2 us
  Pallas kernels  48.4 us (94%)
  local copies, waits for them, and re-layouts  2.77 us (5%)
    pallas_call x1, Pallas kernels, shards(): pl.pallas_call(functools.partial(kernel, nc, nf, nbins), out_shape=jax.Sh...  48.4 us
    reshape x1, local copies, waits for them, and re-layouts, shards(): return jnp.transpose(received, (3, 2, 0, 1, 4)).reshape(fl, 2, nbins, vl)  2.77 us

profile of v3, /device:TPU:1, one launch (start us, length us, event | category | flops | bytes accessed | tf_op | source)
XLA Modules:
  0.0 51.2 jit_solution(10337286970545552881)
XLA Ops:
  0.0 48.4 %shard_map.46 = bf16[8,2,32,1024]{3,2,1,0:T(8,128)(2,1)} custom-call(bf16[2,8,32,256]{3,2,1,0:T(8,128)(2,1)} %rf_ref.1, s32[3,1024]{1,0:T(4,128)} %elem_hbm.1, s32[3,1024]{1,0:T(4,128)} %vox_hbm.1, s32[8]{0:T(128)} %sub_hbm.1), custom_call_target="tpu_custom_call" | custom-call | tf_op jit(solution)/shard_map/pallas_call | solution.py:398
  48.4 2.8 %copy.5 = bf16[32,2,8,1024]{3,2,1,0:T(8,128)(2,1)} copy(bf16[32,2,8,1024]{3,0,1,2:T(8,128)(2,1)} %bitcast.5) | data formatting | bytes 2097152 | tf_op jit(solution)/shard_map/reshape | solution.py:427

commit v4 on v3

--- a/solution.py
+++ b/solution.py
@@ -22,7 +22,7 @@
 )
 LANES = 128
 ROUND = 12582912.0
-GO_AT = 4
+GO_AT = 7
 
 
 def horner(coefs, z):

time: 51.4 us -> 51 us (level)
  no operation moved by 1% of the time
where the time goes in v4:
time: 51 us; the launch traced here: 50.8 us
  Pallas kernels  48 us (94%)
  local copies, waits for them, and re-layouts  2.77 us (5%)
    pallas_call x1, Pallas kernels, shards(): pl.pallas_call(functools.partial(kernel, nc, nf, nbins), out_shape=jax.Sh...  48 us
    reshape x1, local copies, waits for them, and re-layouts, shards(): return jnp.transpose(received, (3, 2, 0, 1, 4)).reshape(fl, 2, nbins, vl)  2.77 us

profile of v4, /device:TPU:1, one launch (start us, length us, event | category | flops | bytes accessed | tf_op | source)
XLA Modules:
  0.0 50.8 jit_solution(7255258466464496696)
XLA Ops:
  0.0 48.0 %shard_map.46 = bf16[8,2,32,1024]{3,2,1,0:T(8,128)(2,1)} custom-call(bf16[2,8,32,256]{3,2,1,0:T(8,128)(2,1)} %rf_ref.1, s32[3,1024]{1,0:T(4,128)} %elem_hbm.1, s32[3,1024]{1,0:T(4,128)} %vox_hbm.1, s32[8]{0:T(128)} %sub_hbm.1), custom_call_target="tpu_custom_call" | custom-call | tf_op jit(solution)/shard_map/pallas_call | solution.py:398
  48.0 2.8 %copy.5 = bf16[32,2,8,1024]{3,2,1,0:T(8,128)(2,1)} copy(bf16[32,2,8,1024]{3,0,1,2:T(8,128)(2,1)} %bitcast.5) | data formatting | bytes 2097152 | tf_op jit(solution)/shard_map/reshape | solution.py:427

commit v5 on v4

--- a/solution.py
+++ b/solution.py
@@ -234,9 +234,9 @@
         unless_second(let_go)
 
     for step in range(1, steps):
-        if step == 1:
+        if step == 2:
             multiply(me_c, first=True)
-        else:
+        if step > 1:
             multiply(block_of(1 - step))
             multiply(block_of(step - 1))
 
@@ -253,9 +253,9 @@
 
             unless_second(lambda: portion_of_operator(step, k))
 
-    if steps == 1:
+    if steps <= 2:
         multiply(me_c, first=True)
-    else:
+    if steps > 1:
         multiply(block_of(1 - steps))
         multiply(block_of(steps - 1))
 

time: 51 us -> 51 us (level)
  no operation moved by 1% of the time
where the time goes in v5:
time: 51 us; the launch traced here: 50.8 us
  Pallas kernels  48 us (94%)
  local copies, waits for them, and re-layouts  2.77 us (5%)
    pallas_call x1, Pallas kernels, shards(): pl.pallas_call(functools.partial(kernel, nc, nf, nbins), out_shape=jax.Sh...  48 us
    reshape x1, local copies, waits for them, and re-layouts, shards(): return jnp.transpose(received, (3, 2, 0, 1, 4)).reshape(fl, 2, nbins, vl)  2.77 us

profile of v5, /device:TPU:1, one launch (start us, length us, event | category | flops | bytes accessed | tf_op | source)
XLA Modules:
  0.0 50.8 jit_solution(16618112349684365973)
XLA Ops:
  0.0 48.0 %shard_map.46 = bf16[8,2,32,1024]{3,2,1,0:T(8,128)(2,1)} custom-call(bf16[2,8,32,256]{3,2,1,0:T(8,128)(2,1)} %rf_ref.1, s32[3,1024]{1,0:T(4,128)} %elem_hbm.1, s32[3,1024]{1,0:T(4,128)} %vox_hbm.1, s32[8]{0:T(128)} %sub_hbm.1), custom_call_target="tpu_custom_call" | custom-call | tf_op jit(solution)/shard_map/pallas_call | solution.py:398
  48.0 2.8 %copy.5 = bf16[32,2,8,1024]{3,2,1,0:T(8,128)(2,1)} copy(bf16[32,2,8,1024]{3,0,1,2:T(8,128)(2,1)} %bitcast.5) | data formatting | bytes 2097152 | tf_op jit(solution)/shard_map/reshape | solution.py:427
